TPU v7x, 512 devices: a whole 4x8x8 slice. The times are simulated.
512 devices in a mesh: dp: 128 (over y, z, core), mp: 4 (over x).
Axes of the slice: x: 4, y: 8, z: 8, core: 2. Of those that a mesh axis runs over, the one named last changes fastest.
Arguments:
- query_hidden: bfloat16 [4096, 32, 768], P('dp', None, 'mp'), may hold values from -6 to 6
- query_proj: bfloat16 [768, 128], P('mp'), may hold values from -0.21875 to 0.21875
- passages: bfloat16 [8192, 128, 128], P(('dp', 'mp')), may hold values from -6 to 6
- teacher: float32 [4096, 4, 64], P('dp'), may hold values from -8 to 8
- neg_blocks: int32 [4096, 4], P('dp'), may hold values from 0 to 127, all different within a row; in each aligned block of 32 rows (0 to 31, 32 to 63, ...) at most 2 rows name the same one
Outputs:
- kl_loss: float32 [4096], P('dp')
Inputs may be any that keep to these rules, and one draw needn't show every extreme that they name: `neg_blocks`: each query names 4 different blocks. Among the 32 queries of one dp index no block is named more than 2 times, and some block is named exactly 2 times.
All inputs are finite; a program needn't handle non-finite values.
Results may differ from a plain program's by a relative error of at most 0.0003.
Values may be sent and summed in bfloat16 or wider, within the bound.
No kernel may reach another device: no remote copies, remote signals or barrier semaphores. Data moves between devices by JAX's collectives and lax.ppermute only.
A program may use at most 64 MiB of HBM per device.

v0:
```python
import jax
import jax.numpy as jnp
from jax import lax
from jax.sharding import PartitionSpec as P

softness = 0.1


def unit_rows(values):
    return values * lax.rsqrt(jnp.sum(values * values, axis=-1, keepdims=True) + 1e-06)


def soft_scores(slot_rows, passage_vecs):
    slot_count = slot_rows.shape[0]
    block_size = 16
    padded_count = -(-slot_count // block_size) * block_size
    blocked = slot_rows.reshape(
        padded_count // block_size, block_size, slot_rows.shape[1], slot_rows.shape[2]
    )

    def block_scores(slot_block):
        sims = jnp.einsum(
            "sie,pje->sipj", slot_block, passage_vecs, preferred_element_type=jnp.float32
        )
        softened = softness * jnp.log(jnp.sum(jnp.exp(sims / softness), axis=-1))
        return jnp.sum(softened, axis=1)

    scored = lax.map(block_scores, blocked)
    return scored.reshape(padded_count, -1)


def per_device(query_hidden, query_proj, passages, teacher, neg_blocks):
    partial_sum = jnp.einsum(
        "qth,he->qte", query_hidden, query_proj, preferred_element_type=jnp.float32
    )
    passage_vecs = unit_rows(passages.astype(jnp.float32)).astype(jnp.bfloat16)
    dp_count = lax.axis_size("dp")
    query_count, pick_count = neg_blocks.shape
    embed_width = partial_sum.shape[2]
    row_count = query_count * pick_count
    capacity = max(2, -(-row_count // dp_count))
    slots_all = dp_count * capacity
    owners = neg_blocks.reshape(row_count)
    owner_hits = (owners[:, None] == jnp.arange(dp_count, dtype=jnp.int32)[None, :]).astype(
        jnp.int32
    )
    earlier = jnp.cumsum(owner_hits, axis=0) - owner_hits
    slot_rank = jnp.sum(earlier * owner_hits, axis=1)
    slot_ids = owners * capacity + slot_rank
    matches = (slot_ids[None, :] == jnp.arange(slots_all, dtype=jnp.int32)[:, None]).astype(
        jnp.int32
    )
    row_query = jnp.arange(row_count, dtype=jnp.int32) // pick_count
    source = jnp.sum(matches * row_query[None, :], axis=1)
    filled = jnp.sum(matches, axis=1)
    projected = lax.psum(partial_sum, "mp")
    query_vecs = unit_rows(projected).astype(jnp.bfloat16)
    tokens = query_vecs.shape[1]
    outgoing = query_vecs[source] * filled[:, None, None].astype(jnp.bfloat16)
    outgoing = outgoing.reshape(dp_count, capacity, tokens, embed_width)
    arrived_items = lax.all_to_all(outgoing, "dp", split_axis=0, concat_axis=0, tiled=True)
    dims_items = arrived_items.shape
    flat_items = arrived_items.reshape(dims_items[0] * dims_items[1], dims_items[2], dims_items[3])
    scores = soft_scores(flat_items, passage_vecs).reshape(dims_items[0], dims_items[1], -1)
    returned = lax.all_to_all(scores, "dp", split_axis=0, concat_axis=0, tiled=True)
    home_scores = returned.reshape(slots_all, -1)[slot_ids].reshape(query_count, pick_count, -1)
    teacher_logp = teacher - jnp.log(jnp.sum(jnp.exp(teacher), axis=(1, 2), keepdims=True))
    student = lax.all_gather(home_scores, "mp", axis=2, tiled=True)
    kl_loss = jnp.sum(jnp.exp(teacher_logp) * (teacher_logp - student), axis=(1, 2)) + jnp.log(
        jnp.sum(jnp.exp(student), axis=(1, 2))
    )
    return kl_loss


def solution(mesh):
    in_specs = (
        P("dp", None, "mp"),
        P("mp", None),
        P(("dp", "mp"), None, None),
        P("dp", None, None),
        P("dp", None),
    )
    out_specs = P("dp")
    return jax.shard_map(
        per_device, mesh=mesh, in_specs=in_specs, out_specs=out_specs, check_vma=False
    )
```

profile of v0, /device:TPU:8, one launch (start us, length us, event | category | flops | bytes accessed | tf_op | source)
XLA Modules:
  0.0 229.7 jit_solution(16609151651576874862)
XLA Ops:
  7.6 1.9 fusion.7
  11.2 57.0 %all-reduce.2.cloned.1.call-done = f32[32,32,128]{2,1,0:T(8,128)} async-done(((f32[32,32,128]{2,1,0:T(8,128)}), f32[32,32,128]{2,1,0:T(8,128)}) %all-reduce.2.cloned.1.call-update) | async-done | bytes 524304 | tf_op jit(solution)/shard_map/psum | solution.py:56
  73.4 14.3 %all-to-all-start = ((bf16[128,2,32,128]{3,2,1,0:T(8,128)(2,1)}), bf16[128,2,32,128]{3,2,1,0:T(8,128)(2,1)S(1)}, u32[]{:S(2)}, u32[]{:S(2)}) async-start(bf16[128,2,32,128]{3,2,1,0:T(8,128)(2,1)} %broadcast_multiply_fusion), calls=%async_computation | async-start | bytes 4194304 | tf_op jit(solution)/shard_map/all_to_all | solution.py:61
  89.8 50.3 %all-to-all-done = bf16[128,2,32,128]{3,2,1,0:T(8,128)(2,1)S(1)} async-done(((bf16[128,2,32,128]{3,2,1,0:T(8,128)(2,1)}), bf16[128,2,32,128]{3,2,1,0:T(8,128)(2,1)S(1)}, u32[]{:S(2)}, u32[]{:S(2)}) %all-to-all-start) | async-done | bytes 2097184 | tf_op jit(solution)/shard_map/all_to_all | solution.py:61
  140.1 49.7 %while.10 = (s32[]{:T(128)}, f32[16,16,16]{2,1,0:T(8,128)}, bf16[16,16,32,128]{3,2,1,0:T(8,128)(2,1)S(1)}, bf16[16,128,128]{2,1,0:T(8,128)(2,1)}, s32[]{:T(128)}) while((s32[]{:T(128)}, f32[16,16,16]{2,1,0:T(8,128)}, bf16[16,16,32,128]{3,2,1,0:T(8,128)(2,1)S(1)}, bf16[16,128,128]{2,1,0:T(8,128)(2,1)}, s32[]{:T(128)}) %tuple.25), condition=%wide.region_11.12_spmd, body=%wide.region_8.11_spmd.sunk | while | flops 270540544 | bytes 731713 | solution.py:28
  140.1 2.4 %exponential_reduce_fusion.4 = f32[16,32,16]{1,2,0:T(8,128)S(1)} fusion(bf16[16,128,128]{2,1,0:T(8,128)(2,1)} %get-tuple-element.78, bf16[16,16,32,128]{3,2,1,0:T(8,128)(2,1)S(1)} %get-tuple-element.77, s32[]{:T(128)} %get-tuple-element.70), kind=kOutput, calls=%fused_computation.2.clone.1 | convolution fusion | flops 270524416 | bytes 688132 | tf_op jit(solution)/shard_map/while/body/eval_jaxpr/sie,pje->sipj/dot_general | solution.py:22
  143.2 2.4 %exponential_reduce_fusion.4 = f32[16,32,16]{1,2,0:T(8,128)S(1)} fusion(bf16[16,128,128]{2,1,0:T(8,128)(2,1)} %get-tuple-element.78, bf16[16,16,32,128]{3,2,1,0:T(8,128)(2,1)S(1)} %get-tuple-element.77, s32[]{:T(128)} %get-tuple-element.70), kind=kOutput, calls=%fused_computation.2.clone.1 | convolution fusion | flops 270524416 | bytes 688132 | tf_op jit(solution)/shard_map/while/body/eval_jaxpr/sie,pje->sipj/dot_general | solution.py:22
  146.3 2.4 %exponential_reduce_fusion.4 = f32[16,32,16]{1,2,0:T(8,128)S(1)} fusion(bf16[16,128,128]{2,1,0:T(8,128)(2,1)} %get-tuple-element.78, bf16[16,16,32,128]{3,2,1,0:T(8,128)(2,1)S(1)} %get-tuple-element.77, s32[]{:T(128)} %get-tuple-element.70), kind=kOutput, calls=%fused_computation.2.clone.1 | convolution fusion | flops 270524416 | bytes 688132 | tf_op jit(solution)/shard_map/while/body/eval_jaxpr/sie,pje->sipj/dot_general | solution.py:22
  149.4 2.4 %exponential_reduce_fusion.4 = f32[16,32,16]{1,2,0:T(8,128)S(1)} fusion(bf16[16,128,128]{2,1,0:T(8,128)(2,1)} %get-tuple-element.78, bf16[16,16,32,128]{3,2,1,0:T(8,128)(2,1)S(1)} %get-tuple-element.77, s32[]{:T(128)} %get-tuple-element.70), kind=kOutput, calls=%fused_computation.2.clone.1 | convolution fusion | flops 270524416 | bytes 688132 | tf_op jit(solution)/shard_map/while/body/eval_jaxpr/sie,pje->sipj/dot_general | solution.py:22
  152.5 2.4 %exponential_reduce_fusion.4 = f32[16,32,16]{1,2,0:T(8,128)S(1)} fusion(bf16[16,128,128]{2,1,0:T(8,128)(2,1)} %get-tuple-element.78, bf16[16,16,32,128]{3,2,1,0:T(8,128)(2,1)S(1)} %get-tuple-element.77, s32[]{:T(128)} %get-tuple-element.70), kind=kOutput, calls=%fused_computation.2.clone.1 | convolution fusion | flops 270524416 | bytes 688132 | tf_op jit(solution)/shard_map/while/body/eval_jaxpr/sie,pje->sipj/dot_general | solution.py:22
  155.6 2.4 %exponential_reduce_fusion.4 = f32[16,32,16]{1,2,0:T(8,128)S(1)} fusion(bf16[16,128,128]{2,1,0:T(8,128)(2,1)} %get-tuple-element.78, bf16[16,16,32,128]{3,2,1,0:T(8,128)(2,1)S(1)} %get-tuple-element.77, s32[]{:T(128)} %get-tuple-element.70), kind=kOutput, calls=%fused_computation.2.clone.1 | convolution fusion | flops 270524416 | bytes 688132 | tf_op jit(solution)/shard_map/while/body/eval_jaxpr/sie,pje->sipj/dot_general | solution.py:22
  158.7 2.4 %exponential_reduce_fusion.4 = f32[16,32,16]{1,2,0:T(8,128)S(1)} fusion(bf16[16,128,128]{2,1,0:T(8,128)(2,1)} %get-tuple-element.78, bf16[16,16,32,128]{3,2,1,0:T(8,128)(2,1)S(1)} %get-tuple-element.77, s32[]{:T(128)} %get-tuple-element.70), kind=kOutput, calls=%fused_computation.2.clone.1 | convolution fusion | flops 270524416 | bytes 688132 | tf_op jit(solution)/shard_map/while/body/eval_jaxpr/sie,pje->sipj/dot_general | solution.py:22
  161.8 2.4 %exponential_reduce_fusion.4 = f32[16,32,16]{1,2,0:T(8,128)S(1)} fusion(bf16[16,128,128]{2,1,0:T(8,128)(2,1)} %get-tuple-element.78, bf16[16,16,32,128]{3,2,1,0:T(8,128)(2,1)S(1)} %get-tuple-element.77, s32[]{:T(128)} %get-tuple-element.70), kind=kOutput, calls=%fused_computation.2.clone.1 | convolution fusion | flops 270524416 | bytes 688132 | tf_op jit(solution)/shard_map/while/body/eval_jaxpr/sie,pje->sipj/dot_general | solution.py:22
  164.9 2.4 %exponential_reduce_fusion.4 = f32[16,32,16]{1,2,0:T(8,128)S(1)} fusion(bf16[16,128,128]{2,1,0:T(8,128)(2,1)} %get-tuple-element.78, bf16[16,16,32,128]{3,2,1,0:T(8,128)(2,1)S(1)} %get-tuple-element.77, s32[]{:T(128)} %get-tuple-element.70), kind=kOutput, calls=%fused_computation.2.clone.1 | convolution fusion | flops 270524416 | bytes 688132 | tf_op jit(solution)/shard_map/while/body/eval_jaxpr/sie,pje->sipj/dot_general | solution.py:22
  168.0 2.4 %exponential_reduce_fusion.4 = f32[16,32,16]{1,2,0:T(8,128)S(1)} fusion(bf16[16,128,128]{2,1,0:T(8,128)(2,1)} %get-tuple-element.78, bf16[16,16,32,128]{3,2,1,0:T(8,128)(2,1)S(1)} %get-tuple-element.77, s32[]{:T(128)} %get-tuple-element.70), kind=kOutput, calls=%fused_computation.2.clone.1 | convolution fusion | flops 270524416 | bytes 688132 | tf_op jit(solution)/shard_map/while/body/eval_jaxpr/sie,pje->sipj/dot_general | solution.py:22
  171.1 2.4 %exponential_reduce_fusion.4 = f32[16,32,16]{1,2,0:T(8,128)S(1)} fusion(bf16[16,128,128]{2,1,0:T(8,128)(2,1)} %get-tuple-element.78, bf16[16,16,32,128]{3,2,1,0:T(8,128)(2,1)S(1)} %get-tuple-element.77, s32[]{:T(128)} %get-tuple-element.70), kind=kOutput, calls=%fused_computation.2.clone.1 | convolution fusion | flops 270524416 | bytes 688132 | tf_op jit(solution)/shard_map/while/body/eval_jaxpr/sie,pje->sipj/dot_general | solution.py:22
  174.2 2.4 %exponential_reduce_fusion.4 = f32[16,32,16]{1,2,0:T(8,128)S(1)} fusion(bf16[16,128,128]{2,1,0:T(8,128)(2,1)} %get-tuple-element.78, bf16[16,16,32,128]{3,2,1,0:T(8,128)(2,1)S(1)} %get-tuple-element.77, s32[]{:T(128)} %get-tuple-element.70), kind=kOutput, calls=%fused_computation.2.clone.1 | convolution fusion | flops 270524416 | bytes 688132 | tf_op jit(solution)/shard_map/while/body/eval_jaxpr/sie,pje->sipj/dot_general | solution.py:22
  177.4 2.4 %exponential_reduce_fusion.4 = f32[16,32,16]{1,2,0:T(8,128)S(1)} fusion(bf16[16,128,128]{2,1,0:T(8,128)(2,1)} %get-tuple-element.78, bf16[16,16,32,128]{3,2,1,0:T(8,128)(2,1)S(1)} %get-tuple-element.77, s32[]{:T(128)} %get-tuple-element.70), kind=kOutput, calls=%fused_computation.2.clone.1 | convolution fusion | flops 270524416 | bytes 688132 | tf_op jit(solution)/shard_map/while/body/eval_jaxpr/sie,pje->sipj/dot_general | solution.py:22
  180.5 2.4 %exponential_reduce_fusion.4 = f32[16,32,16]{1,2,0:T(8,128)S(1)} fusion(bf16[16,128,128]{2,1,0:T(8,128)(2,1)} %get-tuple-element.78, bf16[16,16,32,128]{3,2,1,0:T(8,128)(2,1)S(1)} %get-tuple-element.77, s32[]{:T(128)} %get-tuple-element.70), kind=kOutput, calls=%fused_computation.2.clone.1 | convolution fusion | flops 270524416 | bytes 688132 | tf_op jit(solution)/shard_map/while/body/eval_jaxpr/sie,pje->sipj/dot_general | solution.py:22
  183.6 2.4 %exponential_reduce_fusion.4 = f32[16,32,16]{1,2,0:T(8,128)S(1)} fusion(bf16[16,128,128]{2,1,0:T(8,128)(2,1)} %get-tuple-element.78, bf16[16,16,32,128]{3,2,1,0:T(8,128)(2,1)S(1)} %get-tuple-element.77, s32[]{:T(128)} %get-tuple-element.70), kind=kOutput, calls=%fused_computation.2.clone.1 | convolution fusion | flops 270524416 | bytes 688132 | tf_op jit(solution)/shard_map/while/body/eval_jaxpr/sie,pje->sipj/dot_general | solution.py:22
  186.7 2.4 %exponential_reduce_fusion.4 = f32[16,32,16]{1,2,0:T(8,128)S(1)} fusion(bf16[16,128,128]{2,1,0:T(8,128)(2,1)} %get-tuple-element.78, bf16[16,16,32,128]{3,2,1,0:T(8,128)(2,1)S(1)} %get-tuple-element.77, s32[]{:T(128)} %get-tuple-element.70), kind=kOutput, calls=%fused_computation.2.clone.1 | convolution fusion | flops 270524416 | bytes 688132 | tf_op jit(solution)/shard_map/while/body/eval_jaxpr/sie,pje->sipj/dot_general | solution.py:22
  189.8 7.5 %all-to-all-start.1 = ((f32[128,2,16]{2,1,0:T(2,128)}), f32[128,2,16]{2,1,0:T(2,128)S(1)}, u32[]{:S(2)}, u32[]{:S(2)}) async-start(f32[128,2,16]{2,1,0:T(2,128)} %bitcast.10), calls=%async_computation.1 | async-start | bytes 262144 | tf_op jit(solution)/shard_map/all_to_all | solution.py:65
  197.3 11.9 %all-to-all-done.1 = f32[128,2,16]{2,1,0:T(2,128)S(1)} async-done(((f32[128,2,16]{2,1,0:T(2,128)}), f32[128,2,16]{2,1,0:T(2,128)S(1)}, u32[]{:S(2)}, u32[]{:S(2)}) %all-to-all-start.1) | async-done | bytes 16416 | tf_op jit(solution)/shard_map/all_to_all | solution.py:65
  209.9 12.0 %all_gather.3 = f32[32,4,64]{0,1,2:T(4,128)S(1)} all-gather(f32[32,4,16]{0,1,2:T(4,128)S(1)} %copy.21), channel_id=1, replica_groups=mesh['dp'=128,'mp'=4] {'mp'}, dimensions={2}, use_global_device_ids=true | all-gather | bytes 40960 | tf_op jit(solution)/shard_map/all_gather | solution.py:68
  (75 shorter events, 23.0 us)
Async XLA Ops:
  6.5 1.0 copy-start
  6.5 61.6 %all-reduce.2.cloned.1.call-start = ((), (), s32[]{:S(2)}) async-start(), calls=%async_computation.2 | async-start | bytes 1048576 | tf_op jit(solution)/shard_map/psum | solution.py:56
  73.4 14.3 %copy-start.3 = (s32[32,4]{0,1:T(4,128)S(1)}, s32[32,4]{0,1:T(4,128)}, u32[]{:S(2)}) copy-start(s32[32,4]{0,1:T(4,128)} %param.11) | copy-start | bytes 1540
  73.4 14.5 %copy-start.2 = (f32[32,4,64]{2,1,0:T(4,128)S(1)}, f32[32,4,64]{2,1,0:T(4,128)}, u32[]{:S(2)}) copy-start(f32[32,4,64]{2,1,0:T(4,128)} %param.10) | copy-start | bytes 98308
  73.4 14.9 %copy-start.1 = (bf16[16,128,128]{2,1,0:T(8,128)(2,1)S(1)}, bf16[16,128,128]{2,1,0:T(8,128)(2,1)}, u32[]{:S(2)}) copy-start(bf16[16,128,128]{2,1,0:T(8,128)(2,1)} %param.9) | copy-start | bytes 1572868
  73.4 66.7 %all-to-all-start = ((bf16[128,2,32,128]{3,2,1,0:T(8,128)(2,1)}), bf16[128,2,32,128]{3,2,1,0:T(8,128)(2,1)S(1)}, u32[]{:S(2)}, u32[]{:S(2)}) async-start(bf16[128,2,32,128]{3,2,1,0:T(8,128)(2,1)} %broadcast_multiply_fusion), calls=%async_computation | async-start | bytes 4194304 | tf_op jit(solution)/shard_map/all_to_all | solution.py:61
  189.8 19.4 %all-to-all-start.1 = ((f32[128,2,16]{2,1,0:T(2,128)}), f32[128,2,16]{2,1,0:T(2,128)S(1)}, u32[]{:S(2)}, u32[]{:S(2)}) async-start(f32[128,2,16]{2,1,0:T(2,128)} %bitcast.10), calls=%async_computation.1 | async-start | bytes 262144 | tf_op jit(solution)/shard_map/all_to_all | solution.py:65
Sparse Core Ops, SparseCore 0:
  9.7 58.4 all-reduce.1
where the time goes:
time: 231 us; the launch traced here: 230 us
  waiting for transfers between devices  119 us (52%)
  matrix products  39.9 us (17%)
  starting transfers between devices  21.8 us (9%)
  local copies, waits for them, and re-layouts  13.7 us (6%)
  between operations  13.6 us (6%)
  blocking collectives  12 us (5%)
  other arithmetic  9.3 us (4%)
    psum x1, waiting for transfers between devices, per_device(): projected = lax.psum(partial_sum, 'mp')  57 us
    all_to_all x1, waiting for transfers between devices, per_device(): lax.all_to_all(outgoing, 'dp', split_axis=0, concat_axis=0, tiled=True)  50.3 us
    dot_general x16, matrix products, block_scores(): jnp.einsum('sie,pje->sipj', slot_block, passage_vecs, preferred_element_t...  38 us
    all_to_all x1, starting transfers between devices, per_device(): lax.all_to_all(outgoing, 'dp', split_axis=0, concat_axis=0, tiled=True)  14.3 us
    all_gather x1, blocking collectives, per_device(): student = lax.all_gather(home_scores, 'mp', axis=2, tiled=True)  12 us
    all_to_all x1, waiting for transfers between devices, per_device(): lax.all_to_all(scores, 'dp', split_axis=0, concat_axis=0, tiled=True)  11.9 us
    dynamic_update_slice x16, local copies, waits for them, and re-layouts, soft_scores(): scored = lax.map(block_scores, blocked)  9.63 us
    all_to_all x1, starting transfers between devices, per_device(): lax.all_to_all(scores, 'dp', split_axis=0, concat_axis=0, tiled=True)  7.48 us
  transfers between devices with their start and end apart: 3, of which 3 were waited for; matrix products, arithmetic and copies ran while one was open for 2% of the time, Pallas kernels for 0%

commit v1 on v0

--- a/solution.py
+++ b/solution.py
@@ -53,7 +53,7 @@
     row_query = jnp.arange(row_count, dtype=jnp.int32) // pick_count
     source = jnp.sum(matches * row_query[None, :], axis=1)
     filled = jnp.sum(matches, axis=1)
-    projected = lax.psum(partial_sum, "mp")
+    projected = jnp.sum(lax.all_gather(partial_sum, "mp"), axis=0)
     query_vecs = unit_rows(projected).astype(jnp.bfloat16)
     tokens = query_vecs.shape[1]
     outgoing = query_vecs[source] * filled[:, None, None].astype(jnp.bfloat16)

time: 231 us -> 213 us (0.922)
  waiting for transfers between devices: 119 us -> 101 us
    psum x1 -> x0, waiting for transfers between devices: 57 us -> none  [per_device(): projected = lax.psum(partial_sum, 'mp')]
    all_gather x0 -> x1, waiting for transfers between devices: none -> 39.1 us  [per_device(): projected = jnp.sum(lax.all_gather(partial_sum, 'mp'), axis=0)]
where the time goes in v1:
time: 213 us; the launch traced here: 212 us
  waiting for transfers between devices  101 us (47%)
  matrix products  39.9 us (19%)
  starting transfers between devices  21.8 us (10%)
  local copies, waits for them, and re-layouts  13.7 us (6%)
  between operations  13.6 us (6%)
  blocking collectives  12 us (6%)
  other arithmetic  9.09 us (4%)
    all_to_all x1, waiting for transfers between devices, per_device(): lax.all_to_all(outgoing, 'dp', split_axis=0, concat_axis=0, tiled=True)  50.3 us
    all_gather x1, waiting for transfers between devices, per_device(): projected = jnp.sum(lax.all_gather(partial_sum, 'mp'), axis=0)  39.1 us
    dot_general x16, matrix products, block_scores(): jnp.einsum('sie,pje->sipj', slot_block, passage_vecs, preferred_element_t...  38 us
    all_to_all x1, starting transfers between devices, per_device(): lax.all_to_all(outgoing, 'dp', split_axis=0, concat_axis=0, tiled=True)  14.3 us
    all_gather x1, blocking collectives, per_device(): student = lax.all_gather(home_scores, 'mp', axis=2, tiled=True)  12 us
    all_to_all x1, waiting for transfers between devices, per_device(): lax.all_to_all(scores, 'dp', split_axis=0, concat_axis=0, tiled=True)  11.9 us
    dynamic_update_slice x16, local copies, waits for them, and re-layouts, soft_scores(): scored = lax.map(block_scores, blocked)  9.63 us
    all_to_all x1, starting transfers between devices, per_device(): lax.all_to_all(scores, 'dp', split_axis=0, concat_axis=0, tiled=True)  7.47 us
  transfers between devices with their start and end apart: 3, of which 3 were waited for; matrix products, arithmetic and copies ran while one was open for 2% of the time, Pallas kernels for 0%

profile of v1, /device:TPU:8, one launch (start us, length us, event | category | flops | bytes accessed | tf_op | source)
XLA Modules:
  0.0 211.6 jit_solution(6854126806094070366)
XLA Ops:
  7.6 1.9 fusion.7
  11.2 39.1 %all-gather.3.cloned.1.call-done = f32[128,32,128]{2,1,0:T(8,128)} async-done(((f32[32,32,128]{2,1,0:T(8,128)}), f32[128,32,128]{2,1,0:T(8,128)}) %all-gather.3.cloned.1.call-update) | async-done | bytes 2097168 | tf_op jit(solution)/shard_map/all_gather | solution.py:56
  55.3 14.3 %all-to-all-start = ((bf16[128,2,32,128]{3,2,1,0:T(8,128)(2,1)}), bf16[128,2,32,128]{3,2,1,0:T(8,128)(2,1)S(1)}, u32[]{:S(2)}, u32[]{:S(2)}) async-start(bf16[128,2,32,128]{3,2,1,0:T(8,128)(2,1)} %broadcast_multiply_fusion), calls=%async_computation | async-start | bytes 4194304 | tf_op jit(solution)/shard_map/all_to_all | solution.py:61
  71.7 50.3 %all-to-all-done = bf16[128,2,32,128]{3,2,1,0:T(8,128)(2,1)S(1)} async-done(((bf16[128,2,32,128]{3,2,1,0:T(8,128)(2,1)}), bf16[128,2,32,128]{3,2,1,0:T(8,128)(2,1)S(1)}, u32[]{:S(2)}, u32[]{:S(2)}) %all-to-all-start) | async-done | bytes 2097184 | tf_op jit(solution)/shard_map/all_to_all | solution.py:61
  122.0 49.7 %while.10 = (s32[]{:T(128)}, f32[16,16,16]{2,1,0:T(8,128)}, bf16[16,16,32,128]{3,2,1,0:T(8,128)(2,1)S(1)}, bf16[16,128,128]{2,1,0:T(8,128)(2,1)}, s32[]{:T(128)}) while((s32[]{:T(128)}, f32[16,16,16]{2,1,0:T(8,128)}, bf16[16,16,32,128]{3,2,1,0:T(8,128)(2,1)S(1)}, bf16[16,128,128]{2,1,0:T(8,128)(2,1)}, s32[]{:T(128)}) %tuple.25), condition=%wide.region_11.12_spmd, body=%wide.region_8.11_spmd.sunk | while | flops 270540544 | bytes 731713 | solution.py:28
  122.0 2.4 %exponential_reduce_fusion.4 = f32[16,32,16]{1,2,0:T(8,128)S(1)} fusion(bf16[16,128,128]{2,1,0:T(8,128)(2,1)} %get-tuple-element.78, bf16[16,16,32,128]{3,2,1,0:T(8,128)(2,1)S(1)} %get-tuple-element.77, s32[]{:T(128)} %get-tuple-element.70), kind=kOutput, calls=%fused_computation.2.clone.1 | convolution fusion | flops 270524416 | bytes 688132 | tf_op jit(solution)/shard_map/while/body/eval_jaxpr/sie,pje->sipj/dot_general | solution.py:22
  125.1 2.4 %exponential_reduce_fusion.4 = f32[16,32,16]{1,2,0:T(8,128)S(1)} fusion(bf16[16,128,128]{2,1,0:T(8,128)(2,1)} %get-tuple-element.78, bf16[16,16,32,128]{3,2,1,0:T(8,128)(2,1)S(1)} %get-tuple-element.77, s32[]{:T(128)} %get-tuple-element.70), kind=kOutput, calls=%fused_computation.2.clone.1 | convolution fusion | flops 270524416 | bytes 688132 | tf_op jit(solution)/shard_map/while/body/eval_jaxpr/sie,pje->sipj/dot_general | solution.py:22
  128.2 2.4 %exponential_reduce_fusion.4 = f32[16,32,16]{1,2,0:T(8,128)S(1)} fusion(bf16[16,128,128]{2,1,0:T(8,128)(2,1)} %get-tuple-element.78, bf16[16,16,32,128]{3,2,1,0:T(8,128)(2,1)S(1)} %get-tuple-element.77, s32[]{:T(128)} %get-tuple-element.70), kind=kOutput, calls=%fused_computation.2.clone.1 | convolution fusion | flops 270524416 | bytes 688132 | tf_op jit(solution)/shard_map/while/body/eval_jaxpr/sie,pje->sipj/dot_general | solution.py:22
  131.3 2.4 %exponential_reduce_fusion.4 = f32[16,32,16]{1,2,0:T(8,128)S(1)} fusion(bf16[16,128,128]{2,1,0:T(8,128)(2,1)} %get-tuple-element.78, bf16[16,16,32,128]{3,2,1,0:T(8,128)(2,1)S(1)} %get-tuple-element.77, s32[]{:T(128)} %get-tuple-element.70), kind=kOutput, calls=%fused_computation.2.clone.1 | convolution fusion | flops 270524416 | bytes 688132 | tf_op jit(solution)/shard_map/while/body/eval_jaxpr/sie,pje->sipj/dot_general | solution.py:22
  134.4 2.4 %exponential_reduce_fusion.4 = f32[16,32,16]{1,2,0:T(8,128)S(1)} fusion(bf16[16,128,128]{2,1,0:T(8,128)(2,1)} %get-tuple-element.78, bf16[16,16,32,128]{3,2,1,0:T(8,128)(2,1)S(1)} %get-tuple-element.77, s32[]{:T(128)} %get-tuple-element.70), kind=kOutput, calls=%fused_computation.2.clone.1 | convolution fusion | flops 270524416 | bytes 688132 | tf_op jit(solution)/shard_map/while/body/eval_jaxpr/sie,pje->sipj/dot_general | solution.py:22
  137.5 2.4 %exponential_reduce_fusion.4 = f32[16,32,16]{1,2,0:T(8,128)S(1)} fusion(bf16[16,128,128]{2,1,0:T(8,128)(2,1)} %get-tuple-element.78, bf16[16,16,32,128]{3,2,1,0:T(8,128)(2,1)S(1)} %get-tuple-element.77, s32[]{:T(128)} %get-tuple-element.70), kind=kOutput, calls=%fused_computation.2.clone.1 | convolution fusion | flops 270524416 | bytes 688132 | tf_op jit(solution)/shard_map/while/body/eval_jaxpr/sie,pje->sipj/dot_general | solution.py:22
  140.6 2.4 %exponential_reduce_fusion.4 = f32[16,32,16]{1,2,0:T(8,128)S(1)} fusion(bf16[16,128,128]{2,1,0:T(8,128)(2,1)} %get-tuple-element.78, bf16[16,16,32,128]{3,2,1,0:T(8,128)(2,1)S(1)} %get-tuple-element.77, s32[]{:T(128)} %get-tuple-element.70), kind=kOutput, calls=%fused_computation.2.clone.1 | convolution fusion | flops 270524416 | bytes 688132 | tf_op jit(solution)/shard_map/while/body/eval_jaxpr/sie,pje->sipj/dot_general | solution.py:22
  143.7 2.4 %exponential_reduce_fusion.4 = f32[16,32,16]{1,2,0:T(8,128)S(1)} fusion(bf16[16,128,128]{2,1,0:T(8,128)(2,1)} %get-tuple-element.78, bf16[16,16,32,128]{3,2,1,0:T(8,128)(2,1)S(1)} %get-tuple-element.77, s32[]{:T(128)} %get-tuple-element.70), kind=kOutput, calls=%fused_computation.2.clone.1 | convolution fusion | flops 270524416 | bytes 688132 | tf_op jit(solution)/shard_map/while/body/eval_jaxpr/sie,pje->sipj/dot_general | solution.py:22
  146.9 2.4 %exponential_reduce_fusion.4 = f32[16,32,16]{1,2,0:T(8,128)S(1)} fusion(bf16[16,128,128]{2,1,0:T(8,128)(2,1)} %get-tuple-element.78, bf16[16,16,32,128]{3,2,1,0:T(8,128)(2,1)S(1)} %get-tuple-element.77, s32[]{:T(128)} %get-tuple-element.70), kind=kOutput, calls=%fused_computation.2.clone.1 | convolution fusion | flops 270524416 | bytes 688132 | tf_op jit(solution)/shard_map/while/body/eval_jaxpr/sie,pje->sipj/dot_general | solution.py:22
  150.0 2.4 %exponential_reduce_fusion.4 = f32[16,32,16]{1,2,0:T(8,128)S(1)} fusion(bf16[16,128,128]{2,1,0:T(8,128)(2,1)} %get-tuple-element.78, bf16[16,16,32,128]{3,2,1,0:T(8,128)(2,1)S(1)} %get-tuple-element.77, s32[]{:T(128)} %get-tuple-element.70), kind=kOutput, calls=%fused_computation.2.clone.1 | convolution fusion | flops 270524416 | bytes 688132 | tf_op jit(solution)/shard_map/while/body/eval_jaxpr/sie,pje->sipj/dot_general | solution.py:22
  153.1 2.4 %exponential_reduce_fusion.4 = f32[16,32,16]{1,2,0:T(8,128)S(1)} fusion(bf16[16,128,128]{2,1,0:T(8,128)(2,1)} %get-tuple-element.78, bf16[16,16,32,128]{3,2,1,0:T(8,128)(2,1)S(1)} %get-tuple-element.77, s32[]{:T(128)} %get-tuple-element.70), kind=kOutput, calls=%fused_computation.2.clone.1 | convolution fusion | flops 270524416 | bytes 688132 | tf_op jit(solution)/shard_map/while/body/eval_jaxpr/sie,pje->sipj/dot_general | solution.py:22
  156.2 2.4 %exponential_reduce_fusion.4 = f32[16,32,16]{1,2,0:T(8,128)S(1)} fusion(bf16[16,128,128]{2,1,0:T(8,128)(2,1)} %get-tuple-element.78, bf16[16,16,32,128]{3,2,1,0:T(8,128)(2,1)S(1)} %get-tuple-element.77, s32[]{:T(128)} %get-tuple-element.70), kind=kOutput, calls=%fused_computation.2.clone.1 | convolution fusion | flops 270524416 | bytes 688132 | tf_op jit(solution)/shard_map/while/body/eval_jaxpr/sie,pje->sipj/dot_general | solution.py:22
  159.3 2.4 %exponential_reduce_fusion.4 = f32[16,32,16]{1,2,0:T(8,128)S(1)} fusion(bf16[16,128,128]{2,1,0:T(8,128)(2,1)} %get-tuple-element.78, bf16[16,16,32,128]{3,2,1,0:T(8,128)(2,1)S(1)} %get-tuple-element.77, s32[]{:T(128)} %get-tuple-element.70), kind=kOutput, calls=%fused_computation.2.clone.1 | convolution fusion | flops 270524416 | bytes 688132 | tf_op jit(solution)/shard_map/while/body/eval_jaxpr/sie,pje->sipj/dot_general | solution.py:22
  162.4 2.4 %exponential_reduce_fusion.4 = f32[16,32,16]{1,2,0:T(8,128)S(1)} fusion(bf16[16,128,128]{2,1,0:T(8,128)(2,1)} %get-tuple-element.78, bf16[16,16,32,128]{3,2,1,0:T(8,128)(2,1)S(1)} %get-tuple-element.77, s32[]{:T(128)} %get-tuple-element.70), kind=kOutput, calls=%fused_computation.2.clone.1 | convolution fusion | flops 270524416 | bytes 688132 | tf_op jit(solution)/shard_map/while/body/eval_jaxpr/sie,pje->sipj/dot_general | solution.py:22
  165.5 2.4 %exponential_reduce_fusion.4 = f32[16,32,16]{1,2,0:T(8,128)S(1)} fusion(bf16[16,128,128]{2,1,0:T(8,128)(2,1)} %get-tuple-element.78, bf16[16,16,32,128]{3,2,1,0:T(8,128)(2,1)S(1)} %get-tuple-element.77, s32[]{:T(128)} %get-tuple-element.70), kind=kOutput, calls=%fused_computation.2.clone.1 | convolution fusion | flops 270524416 | bytes 688132 | tf_op jit(solution)/shard_map/while/body/eval_jaxpr/sie,pje->sipj/dot_general | solution.py:22
  168.6 2.4 %exponential_reduce_fusion.4 = f32[16,32,16]{1,2,0:T(8,128)S(1)} fusion(bf16[16,128,128]{2,1,0:T(8,128)(2,1)} %get-tuple-element.78, bf16[16,16,32,128]{3,2,1,0:T(8,128)(2,1)S(1)} %get-tuple-element.77, s32[]{:T(128)} %get-tuple-element.70), kind=kOutput, calls=%fused_computation.2.clone.1 | convolution fusion | flops 270524416 | bytes 688132 | tf_op jit(solution)/shard_map/while/body/eval_jaxpr/sie,pje->sipj/dot_general | solution.py:22
  171.7 7.5 %all-to-all-start.1 = ((f32[128,2,16]{2,1,0:T(2,128)}), f32[128,2,16]{2,1,0:T(2,128)S(1)}, u32[]{:S(2)}, u32[]{:S(2)}) async-start(f32[128,2,16]{2,1,0:T(2,128)} %bitcast.11), calls=%async_computation.1 | async-start | bytes 262144 | tf_op jit(solution)/shard_map/all_to_all | solution.py:65
  179.2 11.9 %all-to-all-done.1 = f32[128,2,16]{2,1,0:T(2,128)S(1)} async-done(((f32[128,2,16]{2,1,0:T(2,128)}), f32[128,2,16]{2,1,0:T(2,128)S(1)}, u32[]{:S(2)}, u32[]{:S(2)}) %all-to-all-start.1) | async-done | bytes 16416 | tf_op jit(solution)/shard_map/all_to_all | solution.py:65
  191.9 12.0 %all_gather.11 = f32[32,4,64]{0,1,2:T(4,128)S(1)} all-gather(f32[32,4,16]{0,1,2:T(4,128)S(1)} %copy.21), channel_id=1, replica_groups=mesh['dp'=128,'mp'=4] {'mp'}, dimensions={2}, use_global_device_ids=true | all-gather | bytes 40960 | tf_op jit(solution)/shard_map/all_gather | solution.py:68
  (76 shorter events, 22.8 us)
Async XLA Ops:
  6.5 1.0 copy-start
  6.5 43.8 %all-gather.3.cloned.1.call-start = ((), (), s32[]{:S(2)}) async-start(), calls=%async_computation.2 | async-start | bytes 2621440 | tf_op jit(solution)/shard_map/all_gather | solution.py:56
  55.3 14.3 %copy-start.3 = (s32[32,4]{0,1:T(4,128)S(1)}, s32[32,4]{0,1:T(4,128)}, u32[]{:S(2)}) copy-start(s32[32,4]{0,1:T(4,128)} %param.11) | copy-start | bytes 1540
  55.3 14.5 %copy-start.2 = (f32[32,4,64]{2,1,0:T(4,128)S(1)}, f32[32,4,64]{2,1,0:T(4,128)}, u32[]{:S(2)}) copy-start(f32[32,4,64]{2,1,0:T(4,128)} %param.10) | copy-start | bytes 98308
  55.3 14.9 %copy-start.1 = (bf16[16,128,128]{2,1,0:T(8,128)(2,1)S(1)}, bf16[16,128,128]{2,1,0:T(8,128)(2,1)}, u32[]{:S(2)}) copy-start(bf16[16,128,128]{2,1,0:T(8,128)(2,1)} %param.9) | copy-start | bytes 1572868
  55.3 66.7 %all-to-all-start = ((bf16[128,2,32,128]{3,2,1,0:T(8,128)(2,1)}), bf16[128,2,32,128]{3,2,1,0:T(8,128)(2,1)S(1)}, u32[]{:S(2)}, u32[]{:S(2)}) async-start(bf16[128,2,32,128]{3,2,1,0:T(8,128)(2,1)} %broadcast_multiply_fusion), calls=%async_computation | async-start | bytes 4194304 | tf_op jit(solution)/shard_map/all_to_all | solution.py:61
  171.7 19.4 %all-to-all-start.1 = ((f32[128,2,16]{2,1,0:T(2,128)}), f32[128,2,16]{2,1,0:T(2,128)S(1)}, u32[]{:S(2)}, u32[]{:S(2)}) async-start(f32[128,2,16]{2,1,0:T(2,128)} %bitcast.11), calls=%async_computation.1 | async-start | bytes 262144 | tf_op jit(solution)/shard_map/all_to_all | solution.py:65
Sparse Core Ops, SparseCore 0:
  9.6 40.6 all-gather.2
